TPU v7x, 128 devices: a whole 4x4x4 slice. The times are simulated.
128 devices in a mesh: row: 16 (over z, x_lo, core), col: 8 (over y, x_hi).
Axes of the slice: x: 4 (x_hi: 2, x_lo: 2; x = x_hi * 2 + x_lo), y: 4, z: 4, core: 2. Of those that a mesh axis runs over, the one named last changes fastest.
Arguments:
- genotypes: bfloat16 [5120, 16384], P(None, ('row', 'col')), may hold values from -5 to 5
- running: float32 [16384, 16, 8, 128], P('row', None, 'col'), as said below
- grid_map: int32 [16], replicated, may hold values from 0 to 15, each once
Outputs:
- factored: float32 [16, 16, 64, 16, 8, 128], P(None, 'row', None, None, 'col')
Inputs may be any that keep to these rules, and one draw needn't show every extreme that they name: running is symmetric, and in its first 128 rows each diagonal entry exceeds the sum of the magnitudes of the row's other entries among the first 128 columns. grid_map holds each of its values once.
All inputs are finite; a program needn't handle non-finite values.
Results may differ from a plain program's by a relative error of at most 0.0003.
Values may be sent and summed in bfloat16 or wider, within the bound.
No kernel may reach another device: no remote copies, remote signals or barrier semaphores. Data moves between devices by JAX's collectives and lax.ppermute only.
A program may use at most 128 MiB of HBM per device.

v0:
```python
import jax
import jax.numpy as jnp
from jax import lax
from jax.sharding import PartitionSpec as P

NB = 128


def broadcast(array, axis, root):
    mine = lax.axis_index(axis) == root
    return lax.psum(jnp.where(mine, array, jnp.zeros_like(array)), axis)


def assemble(trail, row_factor, global_rows, col_index, col_width):
    col_pos = jnp.arange(col_width, dtype=jnp.int32)
    in_panel = jnp.logical_and(col_index == 0, col_pos < NB)
    padded = jnp.pad(row_factor, ((0, 0), (0, col_width - NB)))
    left_part = jnp.where(global_rows[:, None] >= col_pos[None, :], padded, jnp.zeros_like(padded))
    right_part = jnp.where(global_rows[:, None] < NB, jnp.zeros_like(trail), trail)
    return jnp.where(in_panel[None, :], left_part, right_part)


def on_device(genotypes, running, grid_map):
    rows_count = lax.axis_size("row")
    row_index = lax.axis_index("row")
    col_index = lax.axis_index("col")
    snp_count = genotypes.shape[0]
    shard_cols = running.shape[3]
    block_rows = running.shape[0]
    sub_rows = block_rows // rows_count
    col_width = running.shape[1] * shard_cols
    mine_rows = lax.all_gather(genotypes, "col", axis=1, tiled=True)
    product = lax.dot_general(
        mine_rows,
        lax.all_gather(genotypes, "row", axis=1, tiled=True),
        (((0,), (0,)), ((), ())),
        preferred_element_type=jnp.float32,
    )
    updated = running.reshape(block_rows, col_width) + product * (1.0 / snp_count)
    inverse_map = jnp.argsort(grid_map)
    leading = broadcast(updated[:NB, :NB], "row", 0)
    lower_factor = jnp.linalg.cholesky(leading)
    own_factor = lax.linalg.triangular_solve(
        lower_factor, updated[:, :NB], left_side=False, lower=True, transpose_a=True
    )
    factor_block = broadcast(own_factor, "col", 0)
    col_slice = lax.dynamic_slice_in_dim(factor_block, col_index * shard_cols, shard_cols, 0)
    col_factor = lax.all_gather(col_slice, "row", axis=0, tiled=True)
    trail = updated - jnp.dot(factor_block, col_factor.T, precision=lax.Precision.HIGHEST)
    global_rows = row_index * block_rows + jnp.arange(block_rows, dtype=jnp.int32)
    finished = assemble(trail, factor_block, global_rows, col_index, col_width)
    send_tiles = jnp.take(finished.reshape(rows_count, sub_rows, col_width), inverse_map, axis=0)
    result = lax.all_to_all(send_tiles, "row", split_axis=0, concat_axis=0, tiled=True)
    return result.reshape(rows_count, 1, sub_rows, rows_count, 1, shard_cols)


def solution(mesh):
    in_specs = (P(None, ("row", "col")), P("row", None, "col", None), P())
    out_specs = P(None, "row", None, None, "col", None)
    return jax.shard_map(
        on_device, mesh=mesh, in_specs=in_specs, out_specs=out_specs, check_vma=False
    )
```

profile of v0, /device:TPU:1, one launch (start us, length us, event | category | flops | bytes accessed | tf_op | source)
XLA Modules:
  0.0 693.8 jit_solution(15372378671997447707)
XLA Ops:
  6.5 0.0 all-gather.4.cloned.1.call-start
  6.5 0.7 all-gather.4.cloned.1.call-update
  7.3 0.0 all-gather.6.cloned.1.call-start
  7.3 0.7 all-gather.6.cloned.1.call-update
  8.0 0.0 all-reduce.4.cloned.1.call-start
  8.1 136.3 %all-gather.4.cloned.1.call-done = bf16[5120,1024]{1,0:T(8,128)(2,1)} async-done(((bf16[5120,128]{1,0:T(8,128)(2,1)}), bf16[5120,1024]{1,0:T(8,128)(2,1)}) %all-gather.4.cloned.1.call-update) | async-done | bytes 10485776 | tf_op jit(solution)/shard_map/all_gather | solution.py:32
  144.4 118.7 %all-gather.6.cloned.1.call-done = bf16[5120,2048]{1,0:T(8,128)(2,1)} async-done(((bf16[5120,128]{1,0:T(8,128)(2,1)}), bf16[5120,2048]{1,0:T(8,128)(2,1)}) %all-gather.6.cloned.1.call-update) | async-done | bytes 20971536 | tf_op jit(solution)/shard_map/all_gather | solution.py:35
  263.1 0.0 copy-start
  263.1 34.6 %bitcast_add_fusion = f32[1024,2048]{1,0:T(8,128)} fusion(f32[128,8,16,128]{3,2,1,0:T(8,128)} %bitcast.20, bf16[5120,1024]{1,0:T(8,128)(2,1)} %all-gather.4.cloned.1.call-done, bf16[5120,2048]{1,0:T(8,128)(2,1)} %all-gather.6.cloned.1.call-done), kind=kOutput, calls=%fused_computation.1 | convolution fusion | flops 21479030784 | bytes 48234496 | tf_op jit(solution)/shard_map/dot_general | solution.py:33
  297.8 1.5 slice_select_fusion
  299.2 0.0 all-reduce.4.cloned.1.call-update
  299.3 0.2 all-reduce.6.cloned.1.call-start
  299.5 104.5 %all-reduce.4.cloned.1.call-done = f32[128,128]{1,0:T(8,128)} async-done(((f32[128,128]{1,0:T(8,128)}), f32[128,128]{1,0:T(8,128)}) %all-reduce.4.cloned.1.call-update) | async-done | bytes 65552 | tf_op jit(solution)/shard_map/psum | solution.py:11
  404.0 0.9 copy.4
  404.9 0.9 fusion.3
  405.8 11.7 %cholesky.15 = f32[128,128]{1,0:T(8,128)S(1)} custom-call(f32[128,128]{1,0:T(8,128)S(1)} %fusion.3), custom_call_target="Cholesky" | custom-call | tf_op jit(solution)/shard_map/jit(cholesky)/cholesky | solution.py:42
  417.6 0.7 compare_reduce_fusion
  418.3 0.7 fusion.1
  419.0 9.8 %custom-call.6 = f32[1,128,128]{1,2,0:T(8,128)S(1)} custom-call(f32[1,128,128]{2,1,0:T(8,128)S(1)} %fusion.1), custom_call_target="InvertDiagBlocksLowerTriangular" | custom-call | tf_op jit(solution)/shard_map/triangular_solve | solution.py:43
  428.8 2.4 convolution_select_fusion
  431.2 0.0 all-reduce.6.cloned.1.call-update
  431.2 0.3 all-gather.8.cloned.1.call-start
  431.5 81.1 %all-reduce.6.cloned.1.call-done = f32[1024,128]{1,0:T(8,128)} async-done(((f32[1024,128]{1,0:T(8,128)}), f32[1024,128]{1,0:T(8,128)}) %all-reduce.6.cloned.1.call-update) | async-done | bytes 524304 | tf_op jit(solution)/shard_map/psum | solution.py:11
  512.6 1.5 constant_dynamic-slice_fusion
  514.0 0.0 all-gather.8.cloned.1.call-update
  514.1 0.0 copy-done
  514.1 1.2 sort.17
  515.4 34.7 %all-gather.8.cloned.1.call-done = f32[2048,128]{1,0:T(8,128)} async-done(((f32[128,128]{1,0:T(8,128)}), f32[2048,128]{1,0:T(8,128)}) %all-gather.8.cloned.1.call-update) | async-done | bytes 1048592 | tf_op jit(solution)/shard_map/all_gather | solution.py:48
  550.0 13.8 %select_select_fusion = f32[1024,2048]{1,0:T(8,128)} fusion(f32[1024,2048]{1,0:T(8,128)} %bitcast_add_fusion, f32[1024,128]{1,0:T(8,128)} %all-reduce.6.cloned.1.call-done, f32[2048,128]{1,0:T(8,128)} %all-gather.8.cloned.1.call-done, s32[1024]{0:T(1024)S(1)} %iota_add_fusion, pred[1024]{0:T(1024)(128)(4,1)S(1)} %broadcast_compare_fusion, ...), kind=kOutput, calls=%fused_computation.2 | convolution fusion | flops 3231711232 | bytes 18357248 | tf_op jit(solution)/shard_map/dot_general | solution.py:49
  563.8 7.7 %gather_fusion = f32[16,64,2048]{2,1,0:T(8,128)} fusion(f32[16,64,2048]{2,1,0:T(8,128)} %bitcast.19, s32[1024]{0:T(1024)S(1)} %pad_clamp_fusion), kind=kCustom, calls=%fused_computation | custom fusion | bytes 16777280 | tf_op jit(solution)/shard_map/jit(_take)/gather | solution.py:52
  571.5 4.3 broadcast_select_fusion
  575.8 98.0 %all_to_all.5 = f32[16,64,2048]{2,1,0:T(8,128)} all-to-all(f32[16,64,2048]{2,1,0:T(8,128)S(1)} %broadcast_select_fusion), channel_id=1, replica_groups=mesh['row'=16,'col'=8] {'row'}, dimensions={0} | all-to-all | bytes 16777216 | tf_op jit(solution)/shard_map/all_to_all | solution.py:53
  673.8 13.5 %reshape.38 = f32[16,1,64,16,1,128]{5,4,3,2,1,0:T(1,128)} reshape(f32[16,64,2048]{2,1,0:T(8,128)} %all_to_all.5) | data formatting | bytes 16777216 | tf_op jit(solution)/shard_map/reshape | solution.py:54
  (8 shorter events, 0.1 us)
Async XLA Ops:
  6.5 137.8 %all-gather.4.cloned.1.call-start = ((), (), s32[]{:S(2)}) async-start(), calls=%async_computation.1 | async-start | bytes 11796480 | tf_op jit(solution)/shard_map/all_gather | solution.py:32
  7.3 255.9 %all-gather.6.cloned.1.call-start = ((), (), s32[]{:S(2)}) async-start(), calls=%async_computation.2 | async-start | bytes 22282240 | tf_op jit(solution)/shard_map/all_gather | solution.py:35
  8.0 396.0 %all-reduce.4.cloned.1.call-start = ((), (), s32[]{:S(2)}) async-start(), calls=%async_computation.3 | async-start | bytes 131072 | tf_op jit(solution)/shard_map/psum | solution.py:11
  263.1 250.9 %copy-start = (s32[16]{0:T(128)S(1)}, s32[16]{0:T(128)}, u32[]{:S(2)}) copy-start(s32[16]{0:T(128)} %param.5) | copy-start | bytes 196
  299.3 213.3 %all-reduce.6.cloned.1.call-start = ((), (), s32[]{:S(2)}) async-start(), calls=%async_computation.4 | async-start | bytes 1048576 | tf_op jit(solution)/shard_map/psum | solution.py:11
  431.2 118.8 %all-gather.8.cloned.1.call-start = ((), (), s32[]{:S(2)}) async-start(), calls=%async_computation.5 | async-start | bytes 1114112 | tf_op jit(solution)/shard_map/all_gather | solution.py:48
Sparse Core Ops, SparseCore 0:
  9.5 134.8 all-gather.3
  146.0 117.0 all-gather.5
  299.4 104.5 all-reduce.3
  431.3 81.2 all-reduce.5
  514.2 35.8 all-gather.7
where the time goes:
time: 695 us; the launch traced here: 694 us
  waiting for transfers between devices  477 us (69%)
  blocking collectives  98 us (14%)
  matrix products  50.8 us (7%)
  other arithmetic  30.9 us (4%)
  local copies, waits for them, and re-layouts  23.6 us (3%)
  between operations  13.2 us (2%)
    psum x2, waiting for transfers between devices, broadcast(): return lax.psum(jnp.where(mine, array, jnp.zeros_like(array)), axis)  186 us
    all_gather x1, waiting for transfers between devices, on_device(): mine_rows = lax.all_gather(genotypes, 'col', axis=1, tiled=True)  136 us
    all_gather x1, waiting for transfers between devices, on_device(): lax.all_gather(genotypes, 'row', axis=1, tiled=True)  119 us
    all_to_all x1, blocking collectives, on_device(): lax.all_to_all(send_tiles, 'row', split_axis=0, concat_axis=0, tiled=True)  98 us
    all_gather x1, waiting for transfers between devices, on_device(): col_factor = lax.all_gather(col_slice, 'row', axis=0, tiled=True)  34.7 us
    dot_general x1, matrix products, on_device(): lax.dot_general(mine_rows, lax.all_gather(genotypes, 'row', axis=1, tiled...  34.6 us
  transfers between devices with their start and end apart: 5, of which 5 were waited for; matrix products, arithmetic and copies ran while one was open for 0% of the time, Pallas kernels for 0%

commit v1 on v0

--- a/solution.py
+++ b/solution.py
@@ -8,7 +8,7 @@
 
 def broadcast(array, axis, root):
     mine = lax.axis_index(axis) == root
-    return lax.psum(jnp.where(mine, array, jnp.zeros_like(array)), axis)
+    return jnp.sum(lax.all_gather(jnp.where(mine, array, jnp.zeros_like(array)), axis), axis=0)
 
 
 def assemble(trail, row_factor, global_rows, col_index, col_width):

time: 695 us -> 605 us (0.87)
  waiting for transfers between devices: 477 us -> 388 us
    psum x2 -> x0, waiting for transfers between devices: 186 us -> none  [broadcast(): return lax.psum(jnp.where(mine, array, jnp.zeros_like(array)), axis)]
    all_gather x0 -> x2, waiting for transfers between devices: none -> 101 us  [broadcast(): lax.all_gather(jnp.where(mine, array, jnp.zeros_like(array)), axis)]
where the time goes in v1:
time: 605 us; the launch traced here: 604 us
  waiting for transfers between devices  388 us (64%)
  blocking collectives  98 us (16%)
  matrix products  48.7 us (8%)
  other arithmetic  33.8 us (6%)
  local copies, waits for them, and re-layouts  21.9 us (4%)
  between operations  13.3 us (2%)
    all_gather x1, waiting for transfers between devices, on_device(): mine_rows = lax.all_gather(genotypes, 'col', axis=1, tiled=True)  136 us
    all_gather x1, waiting for transfers between devices, on_device(): lax.all_gather(genotypes, 'row', axis=1, tiled=True)  119 us
    all_gather x2, waiting for transfers between devices, broadcast(): lax.all_gather(jnp.where(mine, array, jnp.zeros_like(array)), axis)  101 us
    all_to_all x1, blocking collectives, on_device(): lax.all_to_all(send_tiles, 'row', split_axis=0, concat_axis=0, tiled=True)  98 us
    dot_general x1, matrix products, on_device(): lax.dot_general(mine_rows, lax.all_gather(genotypes, 'row', axis=1, tiled...  34.6 us
    all_gather x1, waiting for transfers between devices, on_device(): col_factor = lax.all_gather(col_slice, 'row', axis=0, tiled=True)  30.2 us
    reshape x1, local copies, waits for them, and re-layouts, on_device(): return result.reshape(rows_count, 1, sub_rows, rows_count, 1, shard_cols)  13.5 us
    another operation x3, other arithmetic, on_device(): lower_factor = jnp.linalg.cholesky(leading)  12.5 us
  transfers between devices with their start and end apart: 5, of which 5 were waited for; matrix products, arithmetic and copies ran while one was open for 0% of the time, Pallas kernels for 0%

profile of v1, /device:TPU:1, one launch (start us, length us, event | category | flops | bytes accessed | tf_op | source)
XLA Modules:
  0.0 604.0 jit_solution(14833847625136259112)
XLA Ops:
  6.5 0.0 all-gather.8.cloned.1.call-start
  6.5 0.7 all-gather.8.cloned.1.call-update
  7.3 0.0 all-gather.10.cloned.1.call-start
  7.3 0.7 all-gather.10.cloned.1.call-update
  8.0 0.0 all-gather.14.cloned.1.call-start
  8.1 136.3 %all-gather.8.cloned.1.call-done = bf16[5120,1024]{1,0:T(8,128)(2,1)} async-done(((bf16[5120,128]{1,0:T(8,128)(2,1)}), bf16[5120,1024]{1,0:T(8,128)(2,1)}) %all-gather.8.cloned.1.call-update) | async-done | bytes 10485776 | tf_op jit(solution)/shard_map/all_gather | solution.py:32
  144.4 118.7 %all-gather.10.cloned.1.call-done = bf16[5120,2048]{1,0:T(8,128)(2,1)} async-done(((bf16[5120,128]{1,0:T(8,128)(2,1)}), bf16[5120,2048]{1,0:T(8,128)(2,1)}) %all-gather.10.cloned.1.call-update) | async-done | bytes 20971536 | tf_op jit(solution)/shard_map/all_gather | solution.py:35
  263.1 34.6 %bitcast_add_fusion = f32[1024,2048]{1,0:T(8,128)} fusion(f32[128,8,16,128]{3,2,1,0:T(8,128)} %bitcast.24, bf16[5120,1024]{1,0:T(8,128)(2,1)} %all-gather.8.cloned.1.call-done, bf16[5120,2048]{1,0:T(8,128)(2,1)} %all-gather.10.cloned.1.call-done), kind=kOutput, calls=%fused_computation.1 | convolution fusion | flops 21479030784 | bytes 48234496 | tf_op jit(solution)/shard_map/dot_general | solution.py:33
  297.7 0.0 copy-start
  297.7 1.5 slice_select_fusion
  299.2 0.0 all-gather.14.cloned.1.call-update
  299.2 0.2 all-gather.16.cloned.1.call-start
  299.5 31.4 %all-gather.14.cloned.1.call-done = f32[2048,128]{1,0:T(8,128)} async-done(((f32[128,128]{1,0:T(8,128)}), f32[2048,128]{1,0:T(8,128)}) %all-gather.14.cloned.1.call-update) | async-done | bytes 1048592 | tf_op jit(solution)/shard_map/all_gather | solution.py:11
  330.9 1.3 reduce_sum.18
  332.1 0.1 copy.5
  332.3 11.7 %cholesky.15 = f32[128,128]{1,0:T(8,128)S(1)} custom-call(f32[128,128]{1,0:T(8,128)S(1)} %fusion.3), custom_call_target="Cholesky" | custom-call | tf_op jit(solution)/shard_map/jit(cholesky)/cholesky | solution.py:42
  344.0 0.7 compare_reduce_fusion
  344.7 0.7 fusion.1
  345.4 9.8 %custom-call.6 = f32[1,128,128]{1,2,0:T(8,128)S(1)} custom-call(f32[1,128,128]{2,1,0:T(8,128)S(1)} %fusion.1), custom_call_target="InvertDiagBlocksLowerTriangular" | custom-call | tf_op jit(solution)/shard_map/triangular_solve | solution.py:43
  355.2 2.4 convolution_select_fusion
  357.7 0.0 all-gather.16.cloned.1.call-update
  357.7 0.0 all-gather.12.cloned.1.call-start
  357.7 69.9 %all-gather.16.cloned.1.call-done = f32[8192,128]{1,0:T(8,128)} async-done(((f32[1024,128]{1,0:T(8,128)}), f32[8192,128]{1,0:T(8,128)}) %all-gather.16.cloned.1.call-update) | async-done | bytes 4194320 | tf_op jit(solution)/shard_map/all_gather | solution.py:11
  427.6 2.4 reduce_sum.19
  430.1 0.6 constant_dynamic-slice_fusion
  430.7 0.0 all-gather.12.cloned.1.call-update
  430.7 0.0 copy-done
  430.7 1.2 sort.17
  432.0 30.2 %all-gather.12.cloned.1.call-done = f32[2048,128]{1,0:T(8,128)} async-done(((f32[128,128]{1,0:T(8,128)}), f32[2048,128]{1,0:T(8,128)}) %all-gather.12.cloned.1.call-update) | async-done | bytes 1048592 | tf_op jit(solution)/shard_map/all_gather | solution.py:48
  462.2 11.7 %select_select_fusion = f32[1024,2048]{1,0:T(8,128)} fusion(f32[1024,2048]{1,0:T(8,128)} %bitcast_add_fusion, f32[1024,128]{1,0:T(8,128)S(1)} %reduce_sum.19, f32[2048,128]{1,0:T(8,128)} %all-gather.12.cloned.1.call-done, s32[1024]{0:T(1024)S(1)} %iota_add_fusion, pred[1024]{0:T(1024)(128)(4,1)S(1)} %broadcast_compare_fusion, pred[2048]{0:T(1024)(128)(4,1)S(1)} %fusion.4), kind=kOutput, calls=%fused_computation.2 | convolution fusion | flops 3231711232 | bytes 18357248 | tf_op jit(solution)/shard_map/dot_general | solution.py:49
  473.9 7.7 %gather_fusion = f32[16,64,2048]{2,1,0:T(8,128)} fusion(f32[16,64,2048]{2,1,0:T(8,128)} %bitcast.21, s32[1024]{0:T(1024)S(1)} %pad_clamp_fusion), kind=kCustom, calls=%fused_computation | custom fusion | bytes 16777280 | tf_op jit(solution)/shard_map/jit(_take)/gather | solution.py:52
  481.6 4.3 broadcast_select_fusion
  486.0 98.0 %all_to_all.5 = f32[16,64,2048]{2,1,0:T(8,128)} all-to-all(f32[16,64,2048]{2,1,0:T(8,128)S(1)} %broadcast_select_fusion), channel_id=1, replica_groups=mesh['row'=16,'col'=8] {'row'}, dimensions={0} | all-to-all | bytes 16777216 | tf_op jit(solution)/shard_map/all_to_all | solution.py:53
  584.0 13.5 %reshape.38 = f32[16,1,64,16,1,128]{5,4,3,2,1,0:T(1,128)} reshape(f32[16,64,2048]{2,1,0:T(8,128)} %all_to_all.5) | data formatting | bytes 16777216 | tf_op jit(solution)/shard_map/reshape | solution.py:54
  (9 shorter events, 0.1 us)
Async XLA Ops:
  6.5 137.8 %all-gather.8.cloned.1.call-start = ((), (), s32[]{:S(2)}) async-start(), calls=%async_computation.1 | async-start | bytes 11796480 | tf_op jit(solution)/shard_map/all_gather | solution.py:32
  7.3 255.9 %all-gather.10.cloned.1.call-start = ((), (), s32[]{:S(2)}) async-start(), calls=%async_computation.2 | async-start | bytes 22282240 | tf_op jit(solution)/shard_map/all_gather | solution.py:35
  8.0 322.8 %all-gather.14.cloned.1.call-start = ((), (), s32[]{:S(2)}) async-start(), calls=%async_computation.4 | async-start | bytes 1114112 | tf_op jit(solution)/shard_map/all_gather | solution.py:11
  297.7 133.0 %copy-start = (s32[16]{0:T(128)S(1)}, s32[16]{0:T(128)}, u32[]{:S(2)}) copy-start(s32[16]{0:T(128)} %param.5) | copy-start | bytes 196
  299.2 128.4 %all-gather.16.cloned.1.call-start = ((), (), s32[]{:S(2)}) async-start(), calls=%async_computation.5 | async-start | bytes 4718592 | tf_op jit(solution)/shard_map/all_gather | solution.py:11
  357.7 104.6 %all-gather.12.cloned.1.call-start = ((), (), s32[]{:S(2)}) async-start(), calls=%async_computation.3 | async-start | bytes 1114112 | tf_op jit(solution)/shard_map/all_gather | solution.py:48
Sparse Core Ops, SparseCore 0:
  9.5 134.8 all-gather.7
  146.0 117.0 all-gather.9
  299.4 31.4 all-gather.13
  357.8 69.7 all-gather.15
  430.8 31.3 all-gather.11
